TPU v7x, 32 devices: a whole 2x2x4 slice. The times are simulated.
32 devices in a mesh: row: 8 (over z, core), col: 4 (over y, x).
Axes of the slice: x: 2, y: 2, z: 4, core: 2. Of those that a mesh axis runs over, the one named last changes fastest.
Arguments:
- features: bfloat16 [64, 512, 512], P(None, 'row', 'col'), may hold values from -60 to 60
- memberships: bfloat16 [16, 512, 512], P(None, 'row', 'col'), may hold values from 0 to 1, as said below
- validity: int32 [512, 512], P('row', 'col'), may hold values 0 or 1
Outputs:
- new_memberships: bfloat16 [16, 512, 512], P(None, 'row', 'col')
- centers: float32 [16, 64], replicated
Inputs may be any that keep to these rules, and one draw needn't show every extreme that they name: memberships are positive and a pixel's memberships over the 16 zones sum to 1 up to rounding.
All inputs are finite; a program needn't handle non-finite values. No bound on the sum of `validity` on one device may be relied on, other than what follows from the above.
Results may differ from a plain program's by a relative error of at most 0.004.
Values may be sent and summed in bfloat16 or wider, within the bound.
No kernel may reach another device: no remote copies, remote signals or barrier semaphores. Data moves between devices by JAX's collectives and lax.ppermute only.
A program may use at most 64 MiB of HBM per device.

v0:
```python
from functools import partial

import jax
import jax.numpy as jnp
from jax import lax
from jax.sharding import PartitionSpec as P

ridge_term = 0.01
penalty_weight = 3.0
cost_offset = 0.05


def padded_2(block, sides, width):
    for axis, dim in sides:
        count = lax.axis_size(axis)
        forward = [(i, i + 1) for i in range(count - 1)]
        backward = [(target, source) for source, target in forward]
        low = lax.ppermute(
            lax.slice_in_dim(block, block.shape[dim] - width, None, axis=dim), axis, forward
        )
        high = lax.ppermute(lax.slice_in_dim(block, 0, width, axis=dim), axis, backward)
        block = jnp.concatenate([low, block, high], axis=dim)
    return block


def zone_moments(flat_features, weight_row):
    scaled = weight_row[None, :] * flat_features
    second_moment = lax.dot_general(
        scaled, scaled, (((1,), (1,)), ((), ())), preferred_element_type=jnp.float32
    )
    first_moment = jnp.dot(scaled, weight_row, preferred_element_type=jnp.float32)
    weight_sum = jnp.sum(jnp.square(weight_row.astype(jnp.float32)))
    return (weight_sum, first_moment, second_moment)


def whitening(covariance):
    dimension = covariance.shape[0]
    factor = jnp.linalg.cholesky(covariance)
    scale_det = jnp.exp(2.0 * jnp.sum(jnp.log(jnp.diagonal(factor))) / dimension)
    identity = jnp.eye(dimension, dtype=jnp.float32)
    inverse = lax.linalg.triangular_solve(factor, identity, left_side=True, lower=True)
    return (jnp.sqrt(scale_det) * inverse).astype(jnp.bfloat16)


def factor_zones(zone_counts, first_moment, second_moment):
    dimension = first_moment.shape[1]
    centers = first_moment / zone_counts[:, None]
    covariance = (
        second_moment / zone_counts[:, None, None] - centers[:, :, None] * centers[:, None, :]
    )
    covariance = covariance + ridge_term * jnp.eye(dimension, dtype=jnp.float32)
    white_mats = lax.map(whitening, covariance)
    white_centers = jnp.einsum(
        "kfg,kg->kf", white_mats.astype(jnp.float32), centers, precision=lax.Precision.HIGHEST
    )
    return (white_mats, white_centers, centers)


def zone_distance(flat_features, zone_pair):
    white_mat, white_center = zone_pair
    projected = jnp.dot(white_mat, flat_features, preferred_element_type=jnp.float32)
    return jnp.sum(jnp.square(projected - white_center[:, None]), axis=0)


def on_device(features, memberships, validity):
    num_bands, tile_rows, tile_cols = features.shape
    num_zones = memberships.shape[0]
    valid_map = validity.astype(jnp.float32)
    member_f = memberships.astype(jnp.float32)
    weights_bf = (member_f * valid_map[None]).astype(jnp.bfloat16)
    flat_features = features.reshape(num_bands, tile_rows * tile_cols)
    flat_weights = weights_bf.reshape(num_zones, tile_rows * tile_cols)
    zone_counts, first_moment, second_moment = lax.map(
        partial(zone_moments, flat_features), flat_weights
    )
    penalty_terms = (valid_map[None] * jnp.square(1.0 - member_f)).astype(jnp.bfloat16)
    stacked = jnp.concatenate([penalty_terms, valid_map[None].astype(jnp.bfloat16)], axis=0)
    padded = padded_2(stacked, (("row", 1), ("col", 2)), 1).astype(jnp.float32)
    neighbours = (
        padded[:, :-2, 1:-1] + padded[:, 2:, 1:-1] + padded[:, 1:-1, :-2] + padded[:, 1:-1, 2:]
    )
    penalty = neighbours[:num_zones] / jnp.maximum(neighbours[num_zones], 1.0)[None]
    zone_counts, first_moment, second_moment = lax.psum(
        (zone_counts, first_moment, second_moment), ("row", "col")
    )
    white_mats, white_centers, centers = factor_zones(zone_counts, first_moment, second_moment)
    distance = lax.map(partial(zone_distance, flat_features), (white_mats, white_centers))
    distance = distance.reshape(num_zones, tile_rows, tile_cols)
    cost_total = distance / num_bands + penalty_weight * penalty + cost_offset
    inverse = 1.0 / cost_total
    new_memberships = (valid_map[None] * inverse / jnp.sum(inverse, axis=0, keepdims=True)).astype(
        jnp.bfloat16
    )
    return (new_memberships, centers)


def solution(mesh):
    return jax.shard_map(
        on_device,
        mesh=mesh,
        in_specs=(P(None, "row", "col"), P(None, "row", "col"), P("row", "col")),
        out_specs=(P(None, "row", "col"), P()),
        check_vma=False,
    )
```

profile of v0, /device:TPU:0, one launch (start us, length us, event | category | flops | bytes accessed | tf_op | source)
XLA Modules:
  0.0 446.7 jit_solution(8878036214428196761)
XLA Ops:
  10.1 46.7 %while.36 = (s32[]{:T(128)}, f32[16]{0:T(128)S(1)}, f32[16,64]{1,0:T(8,128)S(1)}, f32[16,64,64]{1,2,0:T(8,128)}, bf16[16,8192]{1,0:T(8,128)(2,1)S(1)}, /*index=5*/bf16[64,8192]{1,0:T(8,128)(2,1)S(1)}, s32[]{:T(128)}, s32[]{:T(128)}) while((s32[]{:T(128)}, f32[16]{0:T(128)S(1)}, f32[16,64]{1,0:T(8,128)S(1)}, f32[16,64,64]{1,2,0:T(8,128)}, ...), condition=%wide.region_2.3_spmd, body=%wide.region_0.2_spmd.sunk | while | flops 69230592 | bytes 2246001 | solution.py:73
  60.5 43.9 %all-reduce = (f32[16,64]{1,0:T(8,128)S(1)}, f32[16]{0:T(128)S(1)}) all-reduce(f32[16,64]{1,0:T(8,128)S(1)} %get-tuple-element.106, f32[16]{0:T(128)S(1)} %get-tuple-element.105), channel_id=1, replica_groups=mesh['row'=8,'col'=4] {'row','col'}, use_global_device_ids=true, to_apply=%region_5.6 | all-reduce | flops 1040 | bytes 8320 | tf_op jit(solution)/shard_map/psum | solution.py:83
  114.0 8.8 %collective-permute-done.3 = bf16[17,66,1]{2,1,0:T(8,128)(2,1)S(1)} collective-permute-done((bf16[17,66,1]{2,1,0:T(8,128)(2,1)S(1)}, bf16[17,66,1]{2,1,0:T(8,128)(2,1)S(1)}, u32[]{:S(2)}, u32[]{:S(2)}) %collective-permute-start.3) | collective-permute-done | bytes 2276 | tf_op jit(solution)/shard_map/ppermute | solution.py:21
  123.9 65.1 %all-reduce.3.cloned.1.call-done = f32[16,64,64]{1,2,0:T(8,128)} async-done(((f32[16,64,64]{1,2,0:T(8,128)}), f32[16,64,64]{1,2,0:T(8,128)}) %all-reduce.3.cloned.1.call-update) | async-done | bytes 262160 | tf_op jit(solution)/shard_map/psum | solution.py:83
  190.2 237.8 %while.37 = (s32[]{:T(128)}, bf16[16,64,64]{2,1,0:T(8,128)(2,1)S(1)}, f32[16,64,64]{1,2,0:T(8,128)S(1)}, s32[]{:T(128)}, f32[]{:T(128)}) while((s32[]{:T(128)}, bf16[16,64,64]{2,1,0:T(8,128)(2,1)S(1)}, f32[16,64,64]{1,2,0:T(8,128)S(1)}, s32[]{:T(128)}, f32[]{:T(128)}) %tuple.67), condition=%wide.region_10.11_spmd, body=%wide.region_6.10_spmd.sunk | while | flops 3195265 | bytes 231535 | solution.py:52
  190.3 5.8 %cholesky.72 = f32[64,64]{1,0:T(8,128)S(1)} custom-call(f32[64,64]{1,0:T(8,128)S(1)} %fusion.53), custom_call_target="Cholesky" | custom-call | tf_op jit(solution)/shard_map/while/body/eval_jaxpr/jit(cholesky)/cholesky | solution.py:38
  197.7 4.9 %custom-call.22 = f32[1,64,64]{1,2,0:T(8,128)S(1)} custom-call(f32[1,64,64]{2,1,0:T(8,128)S(1)} %get-tuple-element.235), custom_call_target="InvertDiagBlocksLowerTriangular" | custom-call | tf_op jit(solution)/shard_map/while/body/eval_jaxpr/triangular_solve | solution.py:41
  205.2 5.8 %cholesky.72 = f32[64,64]{1,0:T(8,128)S(1)} custom-call(f32[64,64]{1,0:T(8,128)S(1)} %fusion.53), custom_call_target="Cholesky" | custom-call | tf_op jit(solution)/shard_map/while/body/eval_jaxpr/jit(cholesky)/cholesky | solution.py:38
  212.5 4.9 %custom-call.22 = f32[1,64,64]{1,2,0:T(8,128)S(1)} custom-call(f32[1,64,64]{2,1,0:T(8,128)S(1)} %get-tuple-element.235), custom_call_target="InvertDiagBlocksLowerTriangular" | custom-call | tf_op jit(solution)/shard_map/while/body/eval_jaxpr/triangular_solve | solution.py:41
  220.1 5.8 %cholesky.72 = f32[64,64]{1,0:T(8,128)S(1)} custom-call(f32[64,64]{1,0:T(8,128)S(1)} %fusion.53), custom_call_target="Cholesky" | custom-call | tf_op jit(solution)/shard_map/while/body/eval_jaxpr/jit(cholesky)/cholesky | solution.py:38
  227.4 4.9 %custom-call.22 = f32[1,64,64]{1,2,0:T(8,128)S(1)} custom-call(f32[1,64,64]{2,1,0:T(8,128)S(1)} %get-tuple-element.235), custom_call_target="InvertDiagBlocksLowerTriangular" | custom-call | tf_op jit(solution)/shard_map/while/body/eval_jaxpr/triangular_solve | solution.py:41
  234.9 5.8 %cholesky.72 = f32[64,64]{1,0:T(8,128)S(1)} custom-call(f32[64,64]{1,0:T(8,128)S(1)} %fusion.53), custom_call_target="Cholesky" | custom-call | tf_op jit(solution)/shard_map/while/body/eval_jaxpr/jit(cholesky)/cholesky | solution.py:38
  242.2 4.9 %custom-call.22 = f32[1,64,64]{1,2,0:T(8,128)S(1)} custom-call(f32[1,64,64]{2,1,0:T(8,128)S(1)} %get-tuple-element.235), custom_call_target="InvertDiagBlocksLowerTriangular" | custom-call | tf_op jit(solution)/shard_map/while/body/eval_jaxpr/triangular_solve | solution.py:41
  249.8 5.8 %cholesky.72 = f32[64,64]{1,0:T(8,128)S(1)} custom-call(f32[64,64]{1,0:T(8,128)S(1)} %fusion.53), custom_call_target="Cholesky" | custom-call | tf_op jit(solution)/shard_map/while/body/eval_jaxpr/jit(cholesky)/cholesky | solution.py:38
  257.1 4.9 %custom-call.22 = f32[1,64,64]{1,2,0:T(8,128)S(1)} custom-call(f32[1,64,64]{2,1,0:T(8,128)S(1)} %get-tuple-element.235), custom_call_target="InvertDiagBlocksLowerTriangular" | custom-call | tf_op jit(solution)/shard_map/while/body/eval_jaxpr/triangular_solve | solution.py:41
  264.7 5.8 %cholesky.72 = f32[64,64]{1,0:T(8,128)S(1)} custom-call(f32[64,64]{1,0:T(8,128)S(1)} %fusion.53), custom_call_target="Cholesky" | custom-call | tf_op jit(solution)/shard_map/while/body/eval_jaxpr/jit(cholesky)/cholesky | solution.py:38
  279.5 5.8 %cholesky.72 = f32[64,64]{1,0:T(8,128)S(1)} custom-call(f32[64,64]{1,0:T(8,128)S(1)} %fusion.53), custom_call_target="Cholesky" | custom-call | tf_op jit(solution)/shard_map/while/body/eval_jaxpr/jit(cholesky)/cholesky | solution.py:38
  286.8 4.9 %custom-call.22 = f32[1,64,64]{1,2,0:T(8,128)S(1)} custom-call(f32[1,64,64]{2,1,0:T(8,128)S(1)} %get-tuple-element.235), custom_call_target="InvertDiagBlocksLowerTriangular" | custom-call | tf_op jit(solution)/shard_map/while/body/eval_jaxpr/triangular_solve | solution.py:41
  294.4 5.8 %cholesky.72 = f32[64,64]{1,0:T(8,128)S(1)} custom-call(f32[64,64]{1,0:T(8,128)S(1)} %fusion.53), custom_call_target="Cholesky" | custom-call | tf_op jit(solution)/shard_map/while/body/eval_jaxpr/jit(cholesky)/cholesky | solution.py:38
  309.2 5.8 %cholesky.72 = f32[64,64]{1,0:T(8,128)S(1)} custom-call(f32[64,64]{1,0:T(8,128)S(1)} %fusion.53), custom_call_target="Cholesky" | custom-call | tf_op jit(solution)/shard_map/while/body/eval_jaxpr/jit(cholesky)/cholesky | solution.py:38
  316.6 4.9 %custom-call.22 = f32[1,64,64]{1,2,0:T(8,128)S(1)} custom-call(f32[1,64,64]{2,1,0:T(8,128)S(1)} %get-tuple-element.235), custom_call_target="InvertDiagBlocksLowerTriangular" | custom-call | tf_op jit(solution)/shard_map/while/body/eval_jaxpr/triangular_solve | solution.py:41
  324.1 5.8 %cholesky.72 = f32[64,64]{1,0:T(8,128)S(1)} custom-call(f32[64,64]{1,0:T(8,128)S(1)} %fusion.53), custom_call_target="Cholesky" | custom-call | tf_op jit(solution)/shard_map/while/body/eval_jaxpr/jit(cholesky)/cholesky | solution.py:38
  339.0 5.8 %cholesky.72 = f32[64,64]{1,0:T(8,128)S(1)} custom-call(f32[64,64]{1,0:T(8,128)S(1)} %fusion.53), custom_call_target="Cholesky" | custom-call | tf_op jit(solution)/shard_map/while/body/eval_jaxpr/jit(cholesky)/cholesky | solution.py:38
  353.8 5.8 %cholesky.72 = f32[64,64]{1,0:T(8,128)S(1)} custom-call(f32[64,64]{1,0:T(8,128)S(1)} %fusion.53), custom_call_target="Cholesky" | custom-call | tf_op jit(solution)/shard_map/while/body/eval_jaxpr/jit(cholesky)/cholesky | solution.py:38
  361.1 4.9 %custom-call.22 = f32[1,64,64]{1,2,0:T(8,128)S(1)} custom-call(f32[1,64,64]{2,1,0:T(8,128)S(1)} %get-tuple-element.235), custom_call_target="InvertDiagBlocksLowerTriangular" | custom-call | tf_op jit(solution)/shard_map/while/body/eval_jaxpr/triangular_solve | solution.py:41
  368.7 5.8 %cholesky.72 = f32[64,64]{1,0:T(8,128)S(1)} custom-call(f32[64,64]{1,0:T(8,128)S(1)} %fusion.53), custom_call_target="Cholesky" | custom-call | tf_op jit(solution)/shard_map/while/body/eval_jaxpr/jit(cholesky)/cholesky | solution.py:38
  383.6 5.8 %cholesky.72 = f32[64,64]{1,0:T(8,128)S(1)} custom-call(f32[64,64]{1,0:T(8,128)S(1)} %fusion.53), custom_call_target="Cholesky" | custom-call | tf_op jit(solution)/shard_map/while/body/eval_jaxpr/jit(cholesky)/cholesky | solution.py:38
  390.9 4.9 %custom-call.22 = f32[1,64,64]{1,2,0:T(8,128)S(1)} custom-call(f32[1,64,64]{2,1,0:T(8,128)S(1)} %get-tuple-element.235), custom_call_target="InvertDiagBlocksLowerTriangular" | custom-call | tf_op jit(solution)/shard_map/while/body/eval_jaxpr/triangular_solve | solution.py:41
  398.4 5.8 %cholesky.72 = f32[64,64]{1,0:T(8,128)S(1)} custom-call(f32[64,64]{1,0:T(8,128)S(1)} %fusion.53), custom_call_target="Cholesky" | custom-call | tf_op jit(solution)/shard_map/while/body/eval_jaxpr/jit(cholesky)/cholesky | solution.py:38
  413.3 5.8 %cholesky.72 = f32[64,64]{1,0:T(8,128)S(1)} custom-call(f32[64,64]{1,0:T(8,128)S(1)} %fusion.53), custom_call_target="Cholesky" | custom-call | tf_op jit(solution)/shard_map/while/body/eval_jaxpr/jit(cholesky)/cholesky | solution.py:38
  420.6 4.9 %custom-call.22 = f32[1,64,64]{1,2,0:T(8,128)S(1)} custom-call(f32[1,64,64]{2,1,0:T(8,128)S(1)} %get-tuple-element.235), custom_call_target="InvertDiagBlocksLowerTriangular" | custom-call | tf_op jit(solution)/shard_map/while/body/eval_jaxpr/triangular_solve | solution.py:41
  428.5 10.2 %while.38 = (s32[]{:T(128)}, f32[16,8192]{1,0:T(8,128)S(1)}, bf16[16,64,64]{2,1,0:T(8,128)(2,1)S(1)}, bf16[64,8192]{1,0:T(8,128)(2,1)S(1)}, f32[16,64]{1,0:T(8,128)S(1)}, /*index=5*/s32[]{:T(128)}, s32[]{:T(128)}) while((s32[]{:T(128)}, f32[16,8192]{1,0:T(8,128)S(1)}, bf16[16,64,64]{2,1,0:T(8,128)(2,1)S(1)}, ...), condition=%wide.region_13.14_spmd, body=%wide.region_11.13_spmd.sunk | while | flops 68673536 | bytes 1164377 | solution.py:87
  (346 shorter events, 158.0 us)
Async XLA Ops:
  7.2 2.2 copy-start
  7.2 181.8 %all-reduce.3.cloned.1.call-start = ((), (), s32[]{:S(2)}) async-start(), calls=%async_computation | async-start | bytes 1048576 | tf_op jit(solution)/shard_map/psum | solution.py:83
  56.8 47.7 %collective-permute-start = (bf16[17,1,128]{2,1,0:T(2,128)(2,1)S(1)}, bf16[17,1,128]{2,1,0:T(2,128)(2,1)S(1)}, u32[]{:S(2)}, u32[]{:S(2)}) collective-permute-start(bf16[17,1,128]{2,1,0:T(2,128)(2,1)S(1)} %get-tuple-element.147), channel_id=1, source_target_pairs={{0,4},{4,8},{8,12},{12,16},{16,20},{20,24},{24,28},{1,5},{5,9},{9,... | collective-permute-start | bytes 13064 | tf_op jit(solution)/shard_map/ppermute | solution.py:18
  59.2 45.3 %collective-permute-start.1 = (bf16[17,1,128]{2,1,0:T(2,128)(2,1)S(1)}, bf16[17,1,128]{2,1,0:T(2,128)(2,1)S(1)}, u32[]{:S(2)}, u32[]{:S(2)}) collective-permute-start(bf16[17,1,128]{2,1,0:T(2,128)(2,1)S(1)} %get-tuple-element.148), channel_id=1, source_target_pairs={{4,0},{8,4},{12,8},{16,12},{20,16},{24,20},{28,24},{5,1},{9,5},{13... | collective-permute-start | bytes 13064 | tf_op jit(solution)/shard_map/ppermute | solution.py:21
  104.5 323.5 %copy-start.1 = (f32[16,64]{1,0:T(8,128)}, f32[16,64]{1,0:T(8,128)S(1)}, u32[]{:S(2)}) copy-start(f32[16,64]{1,0:T(8,128)S(1)} %broadcast_divide_fusion) | copy-start | bytes 12292
  104.8 9.2 %collective-permute-start.2 = (bf16[17,66,1]{2,1,0:T(8,128)(2,1)S(1)}, bf16[17,66,1]{2,1,0:T(8,128)(2,1)S(1)}, u32[]{:S(2)}, u32[]{:S(2)}) collective-permute-start(bf16[17,66,1]{2,1,0:T(8,128)(2,1)S(1)} %get-tuple-element.143), channel_id=1, source_target_pairs={{0,1},{1,2},{2,3},{4,5},{5,6},{6,7},{8,9},{9,10},{10,11},{12,13},{... | collective-permute-start | bytes 6740 | tf_op jit(solution)/shard_map/ppermute | solution.py:18
  109.0 13.8 %collective-permute-start.3 = (bf16[17,66,1]{2,1,0:T(8,128)(2,1)S(1)}, bf16[17,66,1]{2,1,0:T(8,128)(2,1)S(1)}, u32[]{:S(2)}, u32[]{:S(2)}) collective-permute-start(bf16[17,66,1]{2,1,0:T(8,128)(2,1)S(1)} %get-tuple-element.144), channel_id=1, source_target_pairs={{1,0},{2,1},{3,2},{5,4},{6,5},{7,6},{9,8},{10,9},{11,10},{13,12},{... | collective-permute-start | bytes 6740 | tf_op jit(solution)/shard_map/ppermute | solution.py:21
Sparse Core Ops, SparseCore 0:
  56.9 131.9 all-reduce.2
where the time goes:
time: 447 us
  other arithmetic  222 us (50%)
  waiting for transfers between devices  77.6 us (17%)
  blocking collectives  43.9 us (10%)
  matrix products  33.8 us (8%)
  local copies, waits for them, and re-layouts  32.3 us (7%)
  between operations  14.2 us (3%)
  loops' own time  14.1 us (3%)
  starting transfers between devices  9.22 us (2%)
    another operation x48, other arithmetic, whitening(): factor = jnp.linalg.cholesky(covariance)  106 us
    another operation x32, other arithmetic, whitening(): lax.linalg.triangular_solve(factor, identity, left_side=True, lower=True)  89.5 us
    psum x1, waiting for transfers between devices, on_device(): lax.psum((zone_counts, first_moment, second_moment), ('row', 'col'))  65.1 us
    psum x1, blocking collectives, on_device(): lax.psum((zone_counts, first_moment, second_moment), ('row', 'col'))  43.9 us
    dot_general x16, matrix products, zone_moments(): lax.dot_general(scaled, scaled, (((1,), (1,)), ((), ())), preferred_eleme...  16.5 us
    another operation x1, loops' own time, factor_zones(): white_mats = lax.map(whitening, covariance)  13.3 us
    gather x16, local copies, waits for them, and re-layouts, whitening(): jnp.diagonal(factor)  12.9 us
    dynamic_update_slice x32, local copies, waits for them, and re-layouts, on_device(): lax.map(partial(zone_moments, flat_features), flat_weights)  12.5 us
  transfers between devices with their start and end apart: 5, of which 3 were waited for; matrix products, arithmetic and copies ran while one was open for 0% of the time, Pallas kernels for 0%

commit v1 on v0

v1 whole, which is shorter than its diff:
```python
import functools

import jax
import jax.numpy as jnp
from jax import lax
from jax.experimental import pallas as pl
from jax.experimental.pallas import tpu as pltpu
from jax.sharding import PartitionSpec as P

ridge_term = 0.01
penalty_weight = 3.0
cost_offset = 0.05

F32 = jnp.float32
BF16 = jnp.bfloat16
LANES = 128
GROUP = 8


def full_spec():
    return pl.BlockSpec(memory_space=pltpu.VMEM)


def params(mebibytes):
    return pltpu.CompilerParams(vmem_limit_bytes=mebibytes << 20)


def core_half():
    return lax.rem(lax.axis_index("row"), 2)


def moments_kernel(
    feat_ref, memb_ref, valid_ref,
    keep_ref, send_ref, top_ref, bottom_ref, left_ref, right_ref,
    square_ref, lhs_ref, acc_ref,
):
    zones, rows, cols = memb_ref.shape
    bands = feat_ref.shape[1]
    half = zones // 2
    valid = valid_ref[...].astype(F32)
    lane_col = lax.broadcasted_iota(jnp.int32, (rows, LANES), 1)
    left = jnp.where(lane_col == zones, valid[:, 0:1], 0.0)
    right = jnp.where(lane_col == zones, valid[:, cols - 1 : cols], 0.0)
    top_ref[zones : zones + 1, :] = valid[0:1].astype(BF16)
    bottom_ref[zones : zones + 1, :] = valid[rows - 1 : rows].astype(BF16)
    for k in range(zones):
        member = memb_ref[k].astype(F32)
        weight = member * valid
        square_ref[k] = weight * weight
        term = valid * jnp.square(1.0 - member)
        left = jnp.where(lane_col == k, term[:, 0:1], left)
        right = jnp.where(lane_col == k, term[:, cols - 1 : cols], right)
        top_ref[k : k + 1, :] = term[0:1].astype(BF16)
        bottom_ref[k : k + 1, :] = term[rows - 1 : rows].astype(BF16)
    left_ref[...] = left.astype(BF16)
    right_ref[...] = right.astype(BF16)
    acc_ref[...] = jnp.zeros_like(acc_ref)

    def group_step(g, carry):
        base = pl.multiple_of(g * GROUP, GROUP)
        rhs = []
        for r in range(GROUP):
            tile = feat_ref[base + r]
            rhs.append(tile)
            for k in range(zones):
                row = square_ref[k, pl.ds(base + r, 1), :]
                wide = jnp.broadcast_to(row, (bands, cols)).astype(BF16)
                lhs_ref[k * bands : (k + 1) * bands, r * cols : (r + 1) * cols] = wide * tile
            lhs_ref[zones * bands :, r * cols : (r + 1) * cols] = square_ref[
                :, base + r, :
            ].astype(BF16)
        rhs = jnp.concatenate(rhs, axis=1)
        rhs = jnp.concatenate([rhs, jnp.ones((LANES - bands, GROUP * cols), BF16)], axis=0)
        acc_ref[...] += lax.dot_general(
            lhs_ref[...], rhs, (((1,), (1,)), ((), ())), preferred_element_type=F32
        )
        return carry

    lax.fori_loop(0, rows // GROUP, group_step, 0)

    row_i = lax.broadcasted_iota(jnp.int32, (bands, LANES), 0)
    lane_i = lax.broadcasted_iota(jnp.int32, (bands, LANES), 1)
    means = acc_ref[zones * bands :, :]
    zone_row = lax.broadcasted_iota(jnp.int32, (zones, LANES), 0)
    zone_lane = lax.broadcasted_iota(jnp.int32, (zones, LANES), 1)
    diags = jnp.zeros((zones, LANES), F32)
    for k in range(1, zones, 2):
        block = acc_ref[k * bands : (k + 1) * bands, :]
        diag = jnp.sum(jnp.where(lane_i == row_i, block, 0.0), axis=0, keepdims=True)
        diags = jnp.where(zone_row == k, diag, diags)
    diags = pltpu.roll(diags, bands, 1)
    after = pltpu.roll(means, zones - 1, 0)
    even = jnp.where(zone_lane >= bands + bands // 2, after, means)
    odd = jnp.where(zone_lane >= bands, diags, means)
    extra = jnp.where(lax.rem(zone_row, 2) == 0, even, odd)

    me = core_half()
    for out_ref, h in ((keep_ref, me), (send_ref, 1 - me)):
        for b in range(half // 4):

            def zone_block(q):
                start = pl.multiple_of((h * half + 4 * b + q) * bands, bands)
                return acc_ref[pl.ds(start, bands), :]

            first = jnp.where(lane_i <= row_i, zone_block(0), zone_block(1))
            second = jnp.where(lane_i <= row_i, zone_block(2), zone_block(3))
            out_ref[b * bands : (b + 1) * bands, :] = jnp.where(
                lane_i < bands, first, pltpu.roll(second, bands, 1)
            )
        out_ref[half // 4 * bands :, :] = extra


def factor_kernel(sums_ref, white_ref, centers_ref, mat_ref):
    zones, bands = centers_ref.shape
    half = zones // 2
    base = half // 4 * bands
    extra = sums_ref[base : base + zones, :]
    lane_e = lax.broadcasted_iota(jnp.int32, (zones, LANES), 1)
    row_e = lax.broadcasted_iota(jnp.int32, (zones, LANES), 0)
    even_count = extra[:, bands : bands + 1]
    odd_count = pltpu.roll(
        jnp.broadcast_to(extra[:, bands + bands // 2 : bands + bands // 2 + 1], (zones, LANES)), 1, 0
    )
    counts = jnp.where(lax.rem(row_e, 2) == 0, even_count, odd_count)
    centers_ref[...] = (extra / counts)[:, :bands]

    me = core_half()
    mine = sums_ref[pl.ds(pl.multiple_of(base + me * half, half), half), :]
    row_i = lax.broadcasted_iota(jnp.int32, (bands, LANES), 0)
    lane_i = lax.broadcasted_iota(jnp.int32, (bands, LANES), 1)
    eye = jnp.where(lane_i == row_i, 1.0, 0.0).astype(F32)
    right_eye = jnp.where(lane_i == row_i + bands, 1.0, 0.0).astype(F32)
    mine_t = jnp.transpose(jnp.concatenate([mine, jnp.zeros((LANES - half, LANES), F32)], axis=0))
    packed = sums_ref[0:base, :]
    packed_t = jnp.transpose(packed)
    center_rows = []
    for z in range(half):
        pair, odd = z // 2, z % 2
        b, side = pair // 2, pair % 2
        upper = packed[b * bands : (b + 1) * bands, :]
        lower = packed_t[side * bands : (side + 1) * bands, :]
        if side:
            upper = pltpu.roll(upper, bands, 1)
        if b:
            lower = pltpu.roll(lower, bands, 1)
        count_lane = bands if odd == 0 else bands + bands // 2
        count = mine[z - odd : z - odd + 1, count_lane : count_lane + 1]
        center = mine[z : z + 1, :] / count
        column = mine_t[0:bands, z : z + 1] / count
        if odd == 0:
            second = jnp.where(lane_i <= row_i, upper, lower)
        else:
            diag = pltpu.roll(mine[z : z + 1, :], bands, 1)
            second = jnp.where(lane_i > row_i, upper, lower)
            second = jnp.where(lane_i == row_i, diag, second)
        covariance = second / count - column * center + ridge_term * eye
        mat_ref[z] = jnp.where(lane_i < bands, covariance, right_eye)
        center_rows.append(center)

    sub = lax.broadcasted_iota(jnp.int32, (8, LANES), 0)
    blocks = bands // 8
    for kb in range(blocks):

        def step(j, carry):
            k = kb * 8 + 2 * j
            at_first = jnp.full((8, LANES), k, jnp.int32)
            at_second = at_first + 1
            below_first = sub > 2 * j
            below_second = sub > 2 * j + 1
            pivots = []
            for z in range(half):
                first = jnp.broadcast_to(mat_ref[z, pl.ds(k, 1), :], (8, LANES))
                second = jnp.broadcast_to(mat_ref[z, pl.ds(k + 1, 1), :], (8, LANES))
                pivot = jnp.take_along_axis(first, at_first, axis=1)
                cross = jnp.take_along_axis(first, at_second, axis=1)
                under = jnp.take_along_axis(second, at_first, axis=1)
                corner = jnp.take_along_axis(second, at_second, axis=1)
                ratio = cross / pivot
                first = first / pivot
                second = second - under * first
                second = second / (corner - under * ratio)
                pivots.append((first, second, ratio))
            for z in range(half):
                first, second, ratio = pivots[z]
                for rb in range(kb, blocks):
                    block = mat_ref[z, rb * 8 : (rb + 1) * 8, :]
                    left = jnp.take_along_axis(block, at_first, axis=1)
                    right = jnp.take_along_axis(block, at_second, axis=1) - left * ratio
                    if rb == kb:
                        left = jnp.where(below_first, left, 0.0)
                        right = jnp.where(below_second, right, 0.0)
                    mat_ref[z, rb * 8 : (rb + 1) * 8, :] = block - left * first - right * second
            return carry

        lax.fori_loop(0, 4, step, 0)

    for z in range(half):
        mat = mat_ref[z]
        pivots = jnp.sum(mat * eye, axis=1, keepdims=True)
        log_det = jnp.sum(jnp.log(pivots), axis=0, keepdims=True)
        scale = jnp.exp(0.5 * log_det / bands) * lax.rsqrt(pivots)
        white = pltpu.roll(mat, bands, 1) * scale
        white = jnp.where(lane_i < bands, white, 0.0).astype(BF16)
        shift = -jnp.sum(white.astype(F32) * center_rows[z], axis=1, keepdims=True)
        hi = shift.astype(BF16)
        mid = (shift - hi.astype(F32)).astype(BF16)
        low = (shift - hi.astype(F32) - mid.astype(F32)).astype(BF16)
        tail = jnp.where(lane_i == bands, hi.astype(F32), 0.0)
        tail = jnp.where(lane_i == bands + 1, mid.astype(F32), tail)
        tail = jnp.where(lane_i == bands + 2, low.astype(F32), tail)
        white_ref[z * bands : (z + 1) * bands, :] = (white.astype(F32) + tail).astype(BF16)


def penalty_kernel(memb_ref, valid_ref, above_ref, below_ref, left_ref, right_ref, out_ref):
    zones, rows, cols = memb_ref.shape
    valid = valid_ref[...].astype(F32)
    row_i = lax.broadcasted_iota(jnp.int32, (rows, cols), 0)
    lane_i = lax.broadcasted_iota(jnp.int32, (rows, cols), 1)
    above = above_ref[...].astype(F32)
    below = below_ref[...].astype(F32)
    left = left_ref[...].astype(F32)
    right = right_ref[...].astype(F32)

    def neighbours(x, k):
        up = jnp.where(row_i == 0, above[k : k + 1, :], pltpu.roll(x, 1, 0))
        down = jnp.where(row_i == rows - 1, below[k : k + 1, :], pltpu.roll(x, rows - 1, 0))
        west = jnp.where(lane_i == 0, left[:, k : k + 1], pltpu.roll(x, 1, 1))
        east = jnp.where(lane_i == cols - 1, right[:, k : k + 1], pltpu.roll(x, cols - 1, 1))
        return up + down + west + east

    scale = penalty_weight / jnp.maximum(neighbours(valid, zones), 1.0)
    for k in range(zones):
        member = memb_ref[k].astype(F32)
        term = (valid * jnp.square(1.0 - member)).astype(BF16).astype(F32)
        out_ref[k] = neighbours(term, k) * scale + cost_offset


def update_kernel(
    feat_ref, valid_ref, mine_ref, other_ref, penalty_ref, out_ref, white_ref, part_ref
):
    zones, rows, cols = penalty_ref.shape
    bands = feat_ref.shape[1]
    half = zones // 2
    me = core_half()
    span = half * bands
    white_ref[pl.ds(pl.multiple_of(me * span, span), span), :] = mine_ref[...]
    white_ref[pl.ds(pl.multiple_of((1 - me) * span, span), span), :] = other_ref[...]
    ones = jnp.ones((LANES - bands, 2 * cols), BF16)

    def group_step(g, carry):
        base = pl.multiple_of(g * GROUP, GROUP)
        for t in range(GROUP // 2):
            pixels = jnp.concatenate([feat_ref[base + 2 * t], feat_ref[base + 2 * t + 1]], axis=1)
            pixels = jnp.concatenate([pixels, ones], axis=0)
            projected = jnp.dot(white_ref[...], pixels, preferred_element_type=F32)
            squares = jnp.square(projected).reshape(zones, bands // 8, 8, 2 * cols)
            partial = jnp.sum(squares, axis=1)
            part_ref[:, 2 * t] = partial[:, :, :cols]
            part_ref[:, 2 * t + 1] = partial[:, :, cols:]
        total = jnp.zeros((GROUP, cols), F32)
        inverses = []
        for k in range(zones):
            distance = jnp.sum(part_ref[k], axis=1)
            cost = distance * (1.0 / bands) + penalty_ref[k, pl.ds(base, GROUP), :]
            inverse = 1.0 / cost
            inverses.append(inverse)
            total = total + inverse
        ratio = valid_ref[pl.ds(base, GROUP), :].astype(F32) / total
        for k in range(zones):
            out_ref[k, pl.ds(base, GROUP), :] = (inverses[k] * ratio).astype(BF16)
        return carry

    lax.fori_loop(0, rows // GROUP, group_step, 0)


def swap(value, axis, bit):
    count = lax.axis_size(axis)
    return lax.ppermute(value, axis, [(i, i ^ bit) for i in range(count)])


def shift(value, axis, step):
    count = lax.axis_size(axis)
    return lax.ppermute(
        value, axis, [(i, i + step) for i in range(count) if 0 <= i + step < count]
    )


def on_device(features, memberships, validity):
    bands, rows, cols = features.shape
    zones = memberships.shape[0]
    half = zones // 2
    shape = jax.ShapeDtypeStruct
    pixels = features.transpose(1, 0, 2)
    sums_shape = shape((half // 4 * bands + zones, LANES), F32)
    row_edge = shape((zones + 1, cols), BF16)
    col_edge = shape((rows, LANES), BF16)
    keep, send, top, bottom, left, right = pl.pallas_call(
        moments_kernel,
        out_shape=(sums_shape, sums_shape, row_edge, row_edge, col_edge, col_edge),
        in_specs=[full_spec()] * 3,
        out_specs=(full_spec(),) * 6,
        scratch_shapes=[
            pltpu.VMEM((zones, rows, cols), F32),
            pltpu.VMEM((zones * (bands + 1), GROUP * cols), BF16),
            pltpu.VMEM((zones * (bands + 1), LANES), F32),
        ],
        compiler_params=params(24),
        name="moments",
    )(pixels, memberships, validity)
    sums = keep + swap(send, "row", 1)
    for axis in ("col", "row"):
        bit = 1 if axis == "col" else 2
        while bit < lax.axis_size(axis):
            sums = sums + swap(sums, axis, bit)
            bit *= 2
    above = shift(bottom, "row", 1)
    below = shift(top, "row", -1)
    west = shift(right, "col", 1)
    east = shift(left, "col", -1)
    penalty = pl.pallas_call(
        penalty_kernel,
        out_shape=shape((zones, rows, cols), F32),
        in_specs=[full_spec()] * 6,
        out_specs=full_spec(),
        compiler_params=params(8),
        name="penalty",
    )(memberships, validity, above, below, west, east)
    white, centers = pl.pallas_call(
        factor_kernel,
        out_shape=(shape((half * bands, LANES), BF16), shape((zones, bands), F32)),
        in_specs=[full_spec()],
        out_specs=(full_spec(),) * 2,
        scratch_shapes=[pltpu.VMEM((half, bands, LANES), F32)],
        compiler_params=params(8),
        name="factor",
    )(sums)
    other = swap(white, "row", 1)
    new_memberships = pl.pallas_call(
        update_kernel,
        out_shape=shape((zones, rows, cols), BF16),
        in_specs=[full_spec()] * 5,
        out_specs=full_spec(),
        scratch_shapes=[
            pltpu.VMEM((zones * bands, LANES), BF16),
            pltpu.VMEM((zones, GROUP, 8, cols), F32),
        ],
        compiler_params=params(24),
        name="update",
    )(pixels, validity, white, other, penalty)
    return (new_memberships, centers)


def solution(mesh):
    return jax.shard_map(
        on_device,
        mesh=mesh,
        in_specs=(P(None, "row", "col"), P(None, "row", "col"), P("row", "col")),
        out_specs=(P(None, "row", "col"), P()),
        check_vma=False,
    )
```

time: 447 us -> 60.4 us (0.14)
  the two profiles are of different devices: /device:TPU:0 before, /device:TPU:13 now
where the time goes in v1:
time: 60.4 us; the launch traced here: 60.1 us
  starting transfers between devices  21.8 us (36%)
  Pallas kernels  21.1 us (35%)
  waiting for transfers between devices  14.5 us (24%)
  local copies, waits for them, and re-layouts  1.96 us (3%)
  between operations  0.75 us (1%)
    ppermute x4, starting transfers between devices, shift(): lax.ppermute(value, axis, [(i, i + step) for i in range(count) if 0 <= i...  12.5 us
    ppermute x6, waiting for transfers between devices, swap(): return lax.ppermute(value, axis, [(i, i ^ bit) for i in range(count)])  11.4 us
    ppermute x6, starting transfers between devices, swap(): return lax.ppermute(value, axis, [(i, i ^ bit) for i in range(count)])  9.3 us
    pallas_call x1, Pallas kernels, on_device(): pl.pallas_call(factor_kernel, out_shape=(shape((half * bands, LANES), BF1...  7.58 us
    pallas_call x1, Pallas kernels, on_device(): pl.pallas_call(update_kernel, out_shape=shape((zones, rows, cols), BF16),...  6.57 us
    pallas_call x1, Pallas kernels, on_device(): pl.pallas_call(moments_kernel, out_shape=(sums_shape, sums_shape, row_edg...  6.52 us
    ppermute x4, waiting for transfers between devices, shift(): lax.ppermute(value, axis, [(i, i + step) for i in range(count) if 0 <= i...  3.02 us
    unnamed x5, local copies, waits for them, and re-layouts  1.96 us
  transfers between devices with their start and end apart: 10, of which 6 were waited for; matrix products, arithmetic and copies ran while one was open for 0% of the time, Pallas kernels for 1%

profile of v1, /device:TPU:13, one launch (start us, length us, event | category | flops | bytes accessed | tf_op | source)
XLA Modules:
  0.0 60.1 jit_solution(13713627130437168308)
XLA Ops:
  0.6 0.0 copy-start.1
  0.6 0.0 copy-start
  0.6 1.9 %copy.7 = bf16[64,64,128]{2,0,1:T(8,128)(2,1)S(1)} copy(bf16[64,64,128]{2,1,0:T(8,128)(2,1)} %param.3) | data formatting | bytes 2097152 | tf_op args[0]
  2.6 0.0 copy-done.1
  2.6 0.0 copy-done
  2.6 6.5 %moments.1 = (f32[144,128]{1,0:T(8,128)S(1)}, f32[144,128]{1,0:T(8,128)S(1)}, bf16[17,128]{1,0:T(8,128)(2,1)S(1)}, bf16[17,128]{1,0:T(8,128)(2,1)S(1)}, bf16[64,...) custom-call(bf16[64,64,128]{2,1,0:T(8,128)(2,1)S(1)} %bitcast.3, bf16[16,64,128]{2,1,0:T(8,128)(2,1)S(1)} %copy-done, ...), custom_call_target="tpu_custom_call" | custom-call | tf_op jit(solution)/shard_map/moments/pallas_call | solution.py:297
  9.1 0.7 %collective-permute-start = (f32[144,128]{1,0:T(8,128)S(1)}, f32[144,128]{1,0:T(8,128)S(1)}, u32[]{:S(2)}, u32[]{:S(2)}) collective-permute-start(f32[144,128]{1,0:T(8,128)S(1)} %get-tuple-element.11), channel_id=1, source_target_pairs={{0,4},{4,0},{8,12},{12,8},{16,20},{20,16},{24,28},{28,24},{1,5},{5... | collective-permute-start | bytes 221192 | tf_op jit(solution)/shard_map/ppermute | solution.py:278
  9.9 0.9 %collective-permute-done = f32[144,128]{1,0:T(8,128)S(1)} collective-permute-done((f32[144,128]{1,0:T(8,128)S(1)}, f32[144,128]{1,0:T(8,128)S(1)}, u32[]{:S(2)}, u32[]{:S(2)}) %collective-permute-start) | collective-permute-done | bytes 73760 | tf_op jit(solution)/shard_map/ppermute | solution.py:278
  10.8 1.3 %collective-permute-start.1 = (f32[144,128]{1,0:T(8,128)S(1)}, f32[144,128]{1,0:T(8,128)S(1)}, u32[]{:S(2)}, u32[]{:S(2)}) collective-permute-start(f32[144,128]{1,0:T(8,128)S(1)} %add.15), channel_id=1, source_target_pairs={{0,1},{1,0},{2,3},{3,2},{4,5},{5,4},{6,7},{7,6},{8,9},{9,8},{10,11... | collective-permute-start | bytes 221192 | tf_op jit(solution)/shard_map/ppermute | solution.py:278
  12.1 2.0 %collective-permute-done.1 = f32[144,128]{1,0:T(8,128)S(1)} collective-permute-done((f32[144,128]{1,0:T(8,128)S(1)}, f32[144,128]{1,0:T(8,128)S(1)}, u32[]{:S(2)}, u32[]{:S(2)}) %collective-permute-start.1) | collective-permute-done | bytes 73760 | tf_op jit(solution)/shard_map/ppermute | solution.py:278
  14.1 0.3 collective-permute-start.2
  14.4 3.0 %collective-permute-done.2 = f32[144,128]{1,0:T(8,128)S(1)} collective-permute-done((f32[144,128]{1,0:T(8,128)S(1)}, f32[144,128]{1,0:T(8,128)S(1)}, u32[]{:S(2)}, u32[]{:S(2)}) %collective-permute-start.2) | collective-permute-done | bytes 73760 | tf_op jit(solution)/shard_map/ppermute | solution.py:278
  17.4 0.2 collective-permute-start.3
  17.6 3.0 %collective-permute-done.3 = f32[144,128]{1,0:T(8,128)S(1)} collective-permute-done((f32[144,128]{1,0:T(8,128)S(1)}, f32[144,128]{1,0:T(8,128)S(1)}, u32[]{:S(2)}, u32[]{:S(2)}) %collective-permute-start.3) | collective-permute-done | bytes 73760 | tf_op jit(solution)/shard_map/ppermute | solution.py:278
  20.7 2.4 %collective-permute-start.4 = (f32[144,128]{1,0:T(8,128)S(1)}, f32[144,128]{1,0:T(8,128)S(1)}, u32[]{:S(2)}, u32[]{:S(2)}) collective-permute-start(f32[144,128]{1,0:T(8,128)S(1)} %add.18), channel_id=1, source_target_pairs={{0,16},{4,20},{8,24},{12,28},{16,0},{20,4},{24,8},{28,12},{1,17},{... | collective-permute-start | bytes 221192 | tf_op jit(solution)/shard_map/ppermute | solution.py:278
  23.0 2.5 %collective-permute-done.4 = f32[144,128]{1,0:T(8,128)S(1)} collective-permute-done((f32[144,128]{1,0:T(8,128)S(1)}, f32[144,128]{1,0:T(8,128)S(1)}, u32[]{:S(2)}, u32[]{:S(2)}) %collective-permute-start.4) | collective-permute-done | bytes 73760 | tf_op jit(solution)/shard_map/ppermute | solution.py:278
  25.6 7.6 %factor.1 = (bf16[512,128]{1,0:T(8,128)(2,1)S(1)}, f32[16,64]{1,0:T(8,128)}) custom-call(f32[144,128]{1,0:T(8,128)S(1)} %add.19.sums_ref), custom_call_target="tpu_custom_call" | custom-call | tf_op jit(solution)/shard_map/factor/pallas_call | solution.py:328
  33.2 4.4 %collective-permute-start.5 = (bf16[512,128]{1,0:T(8,128)(2,1)S(1)}, bf16[512,128]{1,0:T(8,128)(2,1)S(1)}, u32[]{:S(2)}, u32[]{:S(2)}) collective-permute-start(bf16[512,128]{1,0:T(8,128)(2,1)S(1)} %get-tuple-element.12.mine_ref), channel_id=1, source_target_pairs={{0,4},{4,0},{8,12},{12,8},{16,20},{20,16},{24,28},{28,24},{1,5},{5... | collective-permute-start | bytes 393224 | tf_op jit(solution)/shard_map/ppermute | solution.py:278
  37.5 3.1 %collective-permute-start.8 = (bf16[64,128]{1,0:T(8,128)(2,1)S(1)}, bf16[64,128]{1,0:T(8,128)(2,1)S(1)}, u32[]{:S(2)}, u32[]{:S(2)}) collective-permute-start(bf16[64,128]{1,0:T(8,128)(2,1)S(1)} %get-tuple-element.15), channel_id=1, source_target_pairs={{0,1},{1,2},{2,3},{4,5},{5,6},{6,7},{8,9},{9,10},{10,11},{12,13},{... | collective-permute-start | bytes 49160 | tf_op jit(solution)/shard_map/ppermute | solution.py:283
  40.7 3.1 %collective-permute-start.9 = (bf16[64,128]{1,0:T(8,128)(2,1)S(1)}, bf16[64,128]{1,0:T(8,128)(2,1)S(1)}, u32[]{:S(2)}, u32[]{:S(2)}) collective-permute-start(bf16[64,128]{1,0:T(8,128)(2,1)S(1)} %get-tuple-element.16), channel_id=1, source_target_pairs={{1,0},{2,1},{3,2},{5,4},{6,5},{7,6},{9,8},{10,9},{11,10},{13,12},{... | collective-permute-start | bytes 49160 | tf_op jit(solution)/shard_map/ppermute | solution.py:283
  43.7 4.4 %collective-permute-start.6 = (bf16[17,128]{1,0:T(8,128)(2,1)S(1)}, bf16[17,128]{1,0:T(8,128)(2,1)S(1)}, u32[]{:S(2)}, u32[]{:S(2)}) collective-permute-start(bf16[17,128]{1,0:T(8,128)(2,1)S(1)} %get-tuple-element.13), channel_id=1, source_target_pairs={{0,4},{4,8},{8,12},{12,16},{16,20},{20,24},{24,28},{1,5},{5,9},{9,... | collective-permute-start | bytes 13064 | tf_op jit(solution)/shard_map/ppermute | solution.py:283
  48.1 1.9 %collective-permute-start.7 = (bf16[17,128]{1,0:T(8,128)(2,1)S(1)}, bf16[17,128]{1,0:T(8,128)(2,1)S(1)}, u32[]{:S(2)}, u32[]{:S(2)}) collective-permute-start(bf16[17,128]{1,0:T(8,128)(2,1)S(1)} %get-tuple-element.14), channel_id=1, source_target_pairs={{4,0},{8,4},{12,8},{16,12},{20,16},{24,20},{28,24},{5,1},{9,5},{13... | collective-permute-start | bytes 13064 | tf_op jit(solution)/shard_map/ppermute | solution.py:283
  50.1 0.0 collective-permute-done.6.above_ref
  50.1 3.0 %collective-permute-done.7.below_ref = bf16[17,128]{1,0:T(8,128)(2,1)S(1)} collective-permute-done((bf16[17,128]{1,0:T(8,128)(2,1)S(1)}, bf16[17,128]{1,0:T(8,128)(2,1)S(1)}, u32[]{:S(2)}, u32[]{:S(2)}) %collective-permute-start.7) | collective-permute-done | bytes 4384 | tf_op jit(solution)/shard_map/ppermute | solution.py:283
  53.1 0.0 collective-permute-done.8.left_ref
  53.1 0.0 collective-permute-done.9.right_ref
  53.1 0.5 penalty.1.penalty_ref
  53.6 0.0 collective-permute-done.5.other_ref
  53.6 6.6 %update.1 = bf16[16,64,128]{2,1,0:T(8,128)(2,1)} custom-call(bf16[64,64,128]{2,1,0:T(8,128)(2,1)S(1)} %bitcast.4, s32[64,128]{1,0:T(8,128)S(1)} %copy-done.1, bf16[512,128]{1,0:T(8,128)(2,1)S(1)} %get-tuple-element.12.mine_ref, bf16[512,128]{1,0:T(8,128)(2,1)S(1)} %collective-permute-done.5.other_ref, f32[16,64,128]{2,1,0:T(8,128)S(1)} %penalty.1.penalty_ref), custom_call_target="tpu_custom_call" | custom-call | tf_op jit(solution)/shard_map/update/pallas_call | solution.py:338
  (5 shorter events, 0.1 us)
Async XLA Ops:
  0.6 2.0 %copy-start.1 = (s32[64,128]{1,0:T(8,128)S(1)}, s32[64,128]{1,0:T(8,128)}, u32[]{:S(2)}) copy-start(s32[64,128]{1,0:T(8,128)} %valid_ref.5) | copy-start | bytes 98308
  0.6 2.0 %copy-start = (bf16[16,64,128]{2,1,0:T(8,128)(2,1)S(1)}, bf16[16,64,128]{2,1,0:T(8,128)(2,1)}, u32[]{:S(2)}) copy-start(bf16[16,64,128]{2,1,0:T(8,128)(2,1)} %memb_ref.3) | copy-start | bytes 786436
  9.1 1.7 %collective-permute-start = (f32[144,128]{1,0:T(8,128)S(1)}, f32[144,128]{1,0:T(8,128)S(1)}, u32[]{:S(2)}, u32[]{:S(2)}) collective-permute-start(f32[144,128]{1,0:T(8,128)S(1)} %get-tuple-element.11), channel_id=1, source_target_pairs={{0,4},{4,0},{8,12},{12,8},{16,20},{20,16},{24,28},{28,24},{1,5},{5... | collective-permute-start | bytes 221192 | tf_op jit(solution)/shard_map/ppermute | solution.py:278
  10.8 3.3 %collective-permute-start.1 = (f32[144,128]{1,0:T(8,128)S(1)}, f32[144,128]{1,0:T(8,128)S(1)}, u32[]{:S(2)}, u32[]{:S(2)}) collective-permute-start(f32[144,128]{1,0:T(8,128)S(1)} %add.15), channel_id=1, source_target_pairs={{0,1},{1,0},{2,3},{3,2},{4,5},{5,4},{6,7},{7,6},{8,9},{9,8},{10,11... | collective-permute-start | bytes 221192 | tf_op jit(solution)/shard_map/ppermute | solution.py:278
  14.1 3.3 %collective-permute-start.2 = (f32[144,128]{1,0:T(8,128)S(1)}, f32[144,128]{1,0:T(8,128)S(1)}, u32[]{:S(2)}, u32[]{:S(2)}) collective-permute-start(f32[144,128]{1,0:T(8,128)S(1)} %add.16), channel_id=1, source_target_pairs={{0,2},{1,3},{2,0},{3,1},{4,6},{5,7},{6,4},{7,5},{8,10},{9,11},{10,... | collective-permute-start | bytes 221192 | tf_op jit(solution)/shard_map/ppermute | solution.py:278
  17.4 3.3 %collective-permute-start.3 = (f32[144,128]{1,0:T(8,128)S(1)}, f32[144,128]{1,0:T(8,128)S(1)}, u32[]{:S(2)}, u32[]{:S(2)}) collective-permute-start(f32[144,128]{1,0:T(8,128)S(1)} %add.17), channel_id=1, source_target_pairs={{0,8},{4,12},{8,0},{12,4},{16,24},{20,28},{24,16},{28,20},{1,9},{5... | collective-permute-start | bytes 221192 | tf_op jit(solution)/shard_map/ppermute | solution.py:278
  20.7 4.9 %collective-permute-start.4 = (f32[144,128]{1,0:T(8,128)S(1)}, f32[144,128]{1,0:T(8,128)S(1)}, u32[]{:S(2)}, u32[]{:S(2)}) collective-permute-start(f32[144,128]{1,0:T(8,128)S(1)} %add.18), channel_id=1, source_target_pairs={{0,16},{4,20},{8,24},{12,28},{16,0},{20,4},{24,8},{28,12},{1,17},{... | collective-permute-start | bytes 221192 | tf_op jit(solution)/shard_map/ppermute | solution.py:278
  33.2 20.4 %collective-permute-start.5 = (bf16[512,128]{1,0:T(8,128)(2,1)S(1)}, bf16[512,128]{1,0:T(8,128)(2,1)S(1)}, u32[]{:S(2)}, u32[]{:S(2)}) collective-permute-start(bf16[512,128]{1,0:T(8,128)(2,1)S(1)} %get-tuple-element.12.mine_ref), channel_id=1, source_target_pairs={{0,4},{4,0},{8,12},{12,8},{16,20},{20,16},{24,28},{28,24},{1,5},{5... | collective-permute-start | bytes 393224 | tf_op jit(solution)/shard_map/ppermute | solution.py:278
  37.5 15.5 %collective-permute-start.8 = (bf16[64,128]{1,0:T(8,128)(2,1)S(1)}, bf16[64,128]{1,0:T(8,128)(2,1)S(1)}, u32[]{:S(2)}, u32[]{:S(2)}) collective-permute-start(bf16[64,128]{1,0:T(8,128)(2,1)S(1)} %get-tuple-element.15), channel_id=1, source_target_pairs={{0,1},{1,2},{2,3},{4,5},{5,6},{6,7},{8,9},{9,10},{10,11},{12,13},{... | collective-permute-start | bytes 49160 | tf_op jit(solution)/shard_map/ppermute | solution.py:283
  40.7 12.4 %collective-permute-start.9 = (bf16[64,128]{1,0:T(8,128)(2,1)S(1)}, bf16[64,128]{1,0:T(8,128)(2,1)S(1)}, u32[]{:S(2)}, u32[]{:S(2)}) collective-permute-start(bf16[64,128]{1,0:T(8,128)(2,1)S(1)} %get-tuple-element.16), channel_id=1, source_target_pairs={{1,0},{2,1},{3,2},{5,4},{6,5},{7,6},{9,8},{10,9},{11,10},{13,12},{... | collective-permute-start | bytes 49160 | tf_op jit(solution)/shard_map/ppermute | solution.py:283
  43.7 6.3 %collective-permute-start.6 = (bf16[17,128]{1,0:T(8,128)(2,1)S(1)}, bf16[17,128]{1,0:T(8,128)(2,1)S(1)}, u32[]{:S(2)}, u32[]{:S(2)}) collective-permute-start(bf16[17,128]{1,0:T(8,128)(2,1)S(1)} %get-tuple-element.13), channel_id=1, source_target_pairs={{0,4},{4,8},{8,12},{12,16},{16,20},{20,24},{24,28},{1,5},{5,9},{9,... | collective-permute-start | bytes 13064 | tf_op jit(solution)/shard_map/ppermute | solution.py:283
  48.1 4.9 %collective-permute-start.7 = (bf16[17,128]{1,0:T(8,128)(2,1)S(1)}, bf16[17,128]{1,0:T(8,128)(2,1)S(1)}, u32[]{:S(2)}, u32[]{:S(2)}) collective-permute-start(bf16[17,128]{1,0:T(8,128)(2,1)S(1)} %get-tuple-element.14), channel_id=1, source_target_pairs={{4,0},{8,4},{12,8},{16,12},{20,16},{24,20},{28,24},{5,1},{9,5},{13... | collective-permute-start | bytes 13064 | tf_op jit(solution)/shard_map/ppermute | solution.py:283
